TPU v7x, 32 devices: a whole 2x2x4 slice. The times are simulated.
32 devices in a mesh: tok: 16 (over z, y, x), col: 2 (over core).
Axes of the slice: x: 2, y: 2, z: 4, core: 2. Of those that a mesh axis runs over, the one named last changes fastest.
Arguments:
- activations: bfloat16 [512, 6144], P('tok', 'col'), may hold values from -61 to 61
- block_slot: int32 [6], replicated, may hold values from 0 to 5, each once
- slot_tile: int32 [32], replicated, may hold values from 0 to 31, each once
Outputs:
- gram_tiles: float32 [32, 1024, 1024], P(('tok', 'col'))
- col_mean: float32 [6144], P('col')
- col_var: float32 [6144], P('col')
Inputs may be any that keep to these rules, and one draw needn't show every extreme that they name: `block_slot`: each stored position once. `slot_tile`: each value once.
All inputs are finite; a program needn't handle non-finite values.
Results may differ from a plain program's by a relative error of at most 0.0003.
Values may be sent and summed in bfloat16 or wider, within the bound.
No kernel may reach another device: no remote copies, remote signals or barrier semaphores. Data moves between devices by JAX's collectives and lax.ppermute only.
A program may use at most 64 MiB of HBM per device.

v0:
```python
import jax
import jax.numpy as jnp
import numpy as np
from jax import lax
from jax.sharding import PartitionSpec as P

BS = 1024


def on_device(activations, block_slot, slot_tile):
    n_tok = lax.axis_size("tok")
    n_col = lax.axis_size("col")
    tok_dev = activations.shape[0]
    total_tokens = tok_dev * n_tok
    col_index = lax.axis_index("col")
    values = activations.astype(jnp.float32)
    col_sum = lax.psum(jnp.sum(values, axis=0), "tok")
    col_mean = col_sum / total_tokens
    squares = lax.psum(jnp.sum((values - col_mean) ** 2, axis=0), "tok")
    col_var = squares / total_tokens
    gathered = lax.all_gather(activations, "col", axis=1, tiled=True)
    block_count = gathered.shape[1] // BS
    pair_count = block_count * (block_count + 1) // 2
    rows_np, cols_np = np.triu_indices(block_count)
    row_table = jnp.asarray(rows_np.astype(np.int32))
    col_table = jnp.asarray(cols_np.astype(np.int32))
    slot_grid = slot_tile.reshape(n_tok, n_col)
    peer_tiles = lax.dynamic_index_in_dim(slot_grid, col_index, 1, keepdims=False)
    clamped = jnp.where(peer_tiles < pair_count, peer_tiles, 0)
    first_slot = block_slot[row_table[clamped]]
    second_slot = block_slot[col_table[clamped]]
    blocks = gathered.reshape(tok_dev, block_count, BS)
    picked = jnp.take(blocks, jnp.stack([first_slot, second_slot], axis=1), axis=1)
    outgoing = picked.transpose(1, 0, 2, 3).reshape(n_tok, tok_dev, 2 * BS)
    arrived = lax.all_to_all(outgoing, "tok", split_axis=0, concat_axis=0, tiled=True)
    arrived = arrived.reshape(n_tok * tok_dev, 2 * BS)
    own_slot = lax.axis_index("tok") * n_col + col_index
    own_tile = lax.dynamic_index_in_dim(slot_tile, own_slot, 0, keepdims=False)
    left_block = arrived[:, :BS]
    right_block = arrived[:, BS:]
    product = (
        lax.dot_general(
            left_block, right_block, (((0,), (0,)), ((), ())), preferred_element_type=jnp.float32
        )
        / total_tokens
    )
    product = jnp.where(own_tile < pair_count, product, jnp.zeros_like(product))
    return (product[None], col_mean, col_var)


def solution(mesh):
    return jax.shard_map(
        on_device,
        mesh=mesh,
        in_specs=(P("tok", "col"), P(), P()),
        out_specs=(P(("tok", "col"), None, None), P("col"), P("col")),
        check_vma=False,
    )
```

profile of v0, /device:TPU:0, one launch (start us, length us, event | category | flops | bytes accessed | tf_op | source)
XLA Modules:
  0.0 200.0 jit_solution(13010305735175130137)
XLA Ops:
  0.6 0.0 copy-start
  0.6 0.0 copy-start.1
  0.7 0.8 reshape.144
  1.4 0.2 fusion.4
  1.6 1.3 gather_fusion
  3.0 0.1 copy.16
  3.0 0.1 fusion.5
  3.2 1.3 gather_fusion.2
  4.5 0.1 copy.19
  4.6 0.1 fusion.6
  4.7 0.0 copy-done
  4.7 0.7 gather_fusion.1
  5.4 0.7 gather_fusion.3
  6.1 0.1 copy.23
  6.1 0.1 reshape.182
  6.3 0.0 copy-done.1
  6.3 2.2 %all_gather.3 = bf16[32,6144]{1,0:T(8,128)(2,1)S(1)} all-gather(bf16[32,3072]{1,0:T(8,128)(2,1)S(1)} %copy-done.1), channel_id=1, replica_groups=mesh['tok'=16,'col'=2] {'col'}, dimensions={1}, use_global_device_ids=true | all-gather | bytes 589824 | tf_op jit(solution)/shard_map/all_gather | solution.py:21
  8.5 0.1 copy.22
  8.6 0.7 gather_fusion.4
  9.3 0.3 select_bitcast_fusion.1
  9.5 1.5 copy.27
  11.1 0.0 copy-start.3
  11.1 8.4 %all-to-all-start = ((bf16[16,32,2048]{2,1,0:T(8,128)(2,1)}), bf16[16,32,2048]{2,1,0:T(8,128)(2,1)S(1)}, u32[]{:S(2)}, u32[]{:S(2)}) async-start(bf16[16,32,2048]{2,1,0:T(8,128)(2,1)} %bitcast.14), calls=%async_computation | async-start | bytes 4194304 | tf_op jit(solution)/shard_map/all_to_all | solution.py:35
  19.5 0.0 copy-done.3
  19.5 0.6 dynamic_slice.8
  20.8 103.5 %psum.14 = f32[3072]{0:T(1024)S(1)} all-reduce(f32[3072]{0:T(1024)S(1)} %convert_reduce_fusion), channel_id=1, replica_groups=mesh['tok'=16,'col'=2] {'tok'}, use_global_device_ids=true, to_apply=%region_1.0 | all-reduce | flops 3072 | bytes 24576 | tf_op jit(solution)/shard_map/psum | solution.py:17
  124.3 0.0 copy-start.2
  124.3 0.1 fusion.3
  124.3 71.7 %psum.15 = f32[3072]{0:T(1024)S(1)} all-reduce(f32[3072]{0:T(1024)S(1)} %fusion.3), channel_id=1, replica_groups=mesh['tok'=16,'col'=2] {'tok'}, use_global_device_ids=true, to_apply=%region_3.0 | all-reduce | flops 3072 | bytes 24576 | tf_op jit(solution)/shard_map/psum | solution.py:19
  196.1 0.6 broadcast_multiply_fusion
  196.7 0.0 all-to-all-done
  196.7 3.3 %select_bitcast_fusion = f32[1,1024,1024]{2,1,0:T(8,128)} fusion(pred[]{:T(512)} %bitcast, bf16[512,2048]{1,0:T(8,128)(2,1)S(1)} %bitcast.23), kind=kOutput, calls=%fused_computation.5 | convolution fusion | flops 1075838976 | bytes 6291457 | tf_op jit(solution)/shard_map/dot_general | solution.py:42
  200.0 0.0 copy-done.2
  (9 shorter events, 0.1 us)
Async XLA Ops:
  0.6 4.1 %copy-start = (s32[6]{0:T(128)S(1)}, s32[6]{0:T(128)}, u32[]{:S(2)}) copy-start(s32[6]{0:T(128)} %param.6) | copy-start | bytes 76
  0.6 5.6 %copy-start.1 = (bf16[32,3072]{1,0:T(8,128)(2,1)S(1)}, bf16[32,3072]{1,0:T(8,128)(2,1)}, u32[]{:S(2)}) copy-start(bf16[32,3072]{1,0:T(8,128)(2,1)} %param.5) | copy-start | bytes 589828
  11.1 8.4 %copy-start.3 = (s32[32]{0:T(128)S(1)}, s32[32]{0:T(128)}, u32[]{:S(2)}) copy-start(s32[32]{0:T(128)} %param.7) | copy-start | bytes 388
  11.1 185.6 %all-to-all-start = ((bf16[16,32,2048]{2,1,0:T(8,128)(2,1)}), bf16[16,32,2048]{2,1,0:T(8,128)(2,1)S(1)}, u32[]{:S(2)}, u32[]{:S(2)}) async-start(bf16[16,32,2048]{2,1,0:T(8,128)(2,1)} %bitcast.14), calls=%async_computation | async-start | bytes 4194304 | tf_op jit(solution)/shard_map/all_to_all | solution.py:35
  124.3 75.7 %copy-start.2 = (f32[3072]{0:T(1024)}, f32[3072]{0:T(1024)S(1)}, u32[]{:S(2)}) copy-start(f32[3072]{0:T(1024)S(1)} %broadcast_multiply_fusion.1) | copy-start | bytes 36868
where the time goes:
time: 200 us
  blocking collectives  177 us (88%)
  starting transfers between devices  8.36 us (4%)
  local copies, waits for them, and re-layouts  8.04 us (4%)
  matrix products  3.31 us (2%)
    psum x1, blocking collectives, on_device(): col_sum = lax.psum(jnp.sum(values, axis=0), 'tok')  103 us
    psum x1, blocking collectives, on_device(): squares = lax.psum(jnp.sum((values - col_mean) ** 2, axis=0), 'tok')  71.7 us
    all_to_all x1, starting transfers between devices, on_device(): lax.all_to_all(outgoing, 'tok', split_axis=0, concat_axis=0, tiled=True)  8.36 us
  transfers between devices with their start and end apart: 1, of which 0 were waited for; matrix products, arithmetic and copies ran while one was open for 1% of the time, Pallas kernels for 0%

commit v1 on v0

--- a/solution.py
+++ b/solution.py
@@ -14,7 +14,7 @@
     total_tokens = tok_dev * n_tok
     col_index = lax.axis_index("col")
     values = activations.astype(jnp.float32)
-    col_sum = lax.psum(jnp.sum(values, axis=0), "tok")
+    col_sum = jnp.sum(lax.all_gather(jnp.sum(values, axis=0), "tok"), axis=0)
     col_mean = col_sum / total_tokens
     squares = lax.psum(jnp.sum((values - col_mean) ** 2, axis=0), "tok")
     col_var = squares / total_tokens

time: 200 us -> 170 us (0.85)
  blocking collectives: 177 us -> 147 us
    psum x1 -> x0, blocking collectives: 103 us -> none  [on_device(): col_sum = lax.psum(jnp.sum(values, axis=0), 'tok')]
    all_gather x0 -> x1, blocking collectives: none -> 69.7 us  [on_device(): col_sum = jnp.sum(lax.all_gather(jnp.sum(values, axis=0), 'tok'), axis=0)]
    psum x1, blocking collectives: 71.7 us -> 75.2 us  [on_device(): squares = lax.psum(jnp.sum((values - col_mean) ** 2, axis=0), 'tok')]
where the time goes in v1:
time: 170 us
  blocking collectives  147 us (86%)
  starting transfers between devices  8.36 us (5%)
  local copies, waits for them, and re-layouts  8.08 us (5%)
  matrix products  3.31 us (2%)
    psum x1, blocking collectives, on_device(): squares = lax.psum(jnp.sum((values - col_mean) ** 2, axis=0), 'tok')  75.2 us
    all_gather x1, blocking collectives, on_device(): col_sum = jnp.sum(lax.all_gather(jnp.sum(values, axis=0), 'tok'), axis=0)  69.7 us
    all_to_all x1, starting transfers between devices, on_device(): lax.all_to_all(outgoing, 'tok', split_axis=0, concat_axis=0, tiled=True)  8.36 us
  transfers between devices with their start and end apart: 1, of which 0 were waited for; matrix products, arithmetic and copies ran while one was open for 1% of the time, Pallas kernels for 0%

profile of v1, /device:TPU:0, one launch (start us, length us, event | category | flops | bytes accessed | tf_op | source)
XLA Modules:
  0.0 169.8 jit_solution(9433689580438644498)
XLA Ops:
  0.6 0.0 copy-start
  0.6 0.0 copy-start.1
  0.7 0.8 reshape.146
  1.4 0.2 fusion.4
  1.6 1.3 gather_fusion
  3.0 0.1 copy.36
  3.0 0.1 fusion.5
  3.2 1.3 gather_fusion.2
  4.5 0.1 copy.39
  4.6 0.1 fusion.6
  4.7 0.0 copy-done
  4.7 0.7 gather_fusion.1
  5.4 0.7 gather_fusion.3
  6.1 0.1 copy.43
  6.1 0.1 reshape.184
  6.3 0.0 copy-done.1
  6.3 2.2 %all_gather.9 = bf16[32,6144]{1,0:T(8,128)(2,1)S(1)} all-gather(bf16[32,3072]{1,0:T(8,128)(2,1)S(1)} %copy-done.1), channel_id=1, replica_groups=mesh['tok'=16,'col'=2] {'col'}, dimensions={1}, use_global_device_ids=true | all-gather | bytes 589824 | tf_op jit(solution)/shard_map/all_gather | solution.py:21
  8.5 0.1 copy.42
  8.6 0.7 gather_fusion.4
  9.3 0.3 select_bitcast_fusion.1
  9.5 1.5 copy.47
  11.1 0.0 copy-start.3
  11.1 8.4 %all-to-all-start = ((bf16[16,32,2048]{2,1,0:T(8,128)(2,1)}), bf16[16,32,2048]{2,1,0:T(8,128)(2,1)S(1)}, u32[]{:S(2)}, u32[]{:S(2)}) async-start(bf16[16,32,2048]{2,1,0:T(8,128)(2,1)} %bitcast.14), calls=%async_computation | async-start | bytes 4194304 | tf_op jit(solution)/shard_map/all_to_all | solution.py:35
  19.5 0.0 copy-done.3
  19.5 0.6 dynamic_slice.8
  20.1 69.7 %all-gather = f32[49152]{0:T(1024)S(1)} all-gather(f32[3072]{0:T(1024)S(1)} %convert_reduce_fusion), channel_id=2, replica_groups=mesh['tok'=16,'col'=2] {'tok'}, dimensions={0}, use_global_device_ids=true | all-gather | bytes 208896 | tf_op jit(solution)/shard_map/all_gather | solution.py:17
  90.6 0.0 copy-start.2
  90.6 0.1 fusion.3
  90.7 75.2 %psum.7 = f32[3072]{0:T(1024)S(1)} all-reduce(f32[3072]{0:T(1024)S(1)} %fusion.3), channel_id=1, replica_groups=mesh['tok'=16,'col'=2] {'tok'}, use_global_device_ids=true, to_apply=%region_3.0 | all-reduce | flops 3072 | bytes 24576 | tf_op jit(solution)/shard_map/psum | solution.py:19
  165.8 0.6 broadcast_multiply_fusion
  166.4 0.0 all-to-all-done
  166.4 3.3 %select_bitcast_fusion = f32[1,1024,1024]{2,1,0:T(8,128)} fusion(pred[]{:T(512)} %bitcast, bf16[512,2048]{1,0:T(8,128)(2,1)S(1)} %bitcast.23), kind=kOutput, calls=%fused_computation.5 | convolution fusion | flops 1075838976 | bytes 6291457 | tf_op jit(solution)/shard_map/dot_general | solution.py:42
  169.8 0.0 copy-done.2
  (11 shorter events, 0.2 us)
Async XLA Ops:
  0.6 4.1 %copy-start = (s32[6]{0:T(128)S(1)}, s32[6]{0:T(128)}, u32[]{:S(2)}) copy-start(s32[6]{0:T(128)} %param.6) | copy-start | bytes 76
  0.6 5.6 %copy-start.1 = (bf16[32,3072]{1,0:T(8,128)(2,1)S(1)}, bf16[32,3072]{1,0:T(8,128)(2,1)}, u32[]{:S(2)}) copy-start(bf16[32,3072]{1,0:T(8,128)(2,1)} %param.5) | copy-start | bytes 589828
  11.1 8.4 %copy-start.3 = (s32[32]{0:T(128)S(1)}, s32[32]{0:T(128)}, u32[]{:S(2)}) copy-start(s32[32]{0:T(128)} %param.7) | copy-start | bytes 388
  11.1 155.4 %all-to-all-start = ((bf16[16,32,2048]{2,1,0:T(8,128)(2,1)}), bf16[16,32,2048]{2,1,0:T(8,128)(2,1)S(1)}, u32[]{:S(2)}, u32[]{:S(2)}) async-start(bf16[16,32,2048]{2,1,0:T(8,128)(2,1)} %bitcast.14), calls=%async_computation | async-start | bytes 4194304 | tf_op jit(solution)/shard_map/all_to_all | solution.py:35
  90.6 79.2 %copy-start.2 = (f32[3072]{0:T(1024)}, f32[3072]{0:T(1024)S(1)}, u32[]{:S(2)}) copy-start(f32[3072]{0:T(1024)S(1)} %broadcast_multiply_fusion.1) | copy-start | bytes 36868
